TPU v7x, 32 devices: a whole 2x2x4 slice. The times are simulated.
32 devices in a mesh: rows: 16 (over z, y, x), heads: 2 (over core).
Axes of the slice: x: 2, y: 2, z: 4, core: 2. Of those that a mesh axis runs over, the one named last changes fastest.
Arguments:
- tokens: bfloat16 [49152, 768], P('rows'), may hold values from -6 to 6
- cotangent: bfloat16 [49152, 768], P(('rows', 'heads')), may hold values from -6 to 6
- lengths: int32 [96], P('rows'), may hold values from 1 to 512, 29491 in all
- qkv_weight: float32 [3, 768, 768], P(None, 'rows', 'heads'), may hold values from -0.3125 to 0.3125
- qkv_first: float32 [3, 768, 768], P(None, 'rows', 'heads'), may hold values from -0.0625 to 0.0625
- qkv_second: float32 [3, 768, 768], P(None, 'rows', 'heads'), may hold values from 1.4e-06 to 5.7e-06
- out_weight: float32 [768, 768], P(('rows', 'heads')), may hold values from -0.625 to 0.625
- out_first: float32 [768, 768], P(('rows', 'heads')), may hold values from -0.0625 to 0.0625
- out_second: float32 [768, 768], P(('rows', 'heads')), may hold values from 1.4e-06 to 5.7e-06
- in_weight: float32 [768, 3072], P(('rows', 'heads')), may hold values from -0.21875 to 0.21875
- in_first: float32 [768, 3072], P(('rows', 'heads')), may hold values from -0.0625 to 0.0625
- in_second: float32 [768, 3072], P(('rows', 'heads')), may hold values from 1.4e-06 to 5.7e-06
- back_weight: float32 [3072, 768], P(('rows', 'heads')), may hold values from -0.109375 to 0.109375
- back_first: float32 [3072, 768], P(('rows', 'heads')), may hold values from -0.0625 to 0.0625
- back_second: float32 [3072, 768], P(('rows', 'heads')), may hold values from 1.4e-06 to 5.7e-06
- vectors: float32 [12, 768], replicated, may hold values from -0.8 to 1.8, as said below
- vector_first: float32 [12, 768], replicated, may hold values from -0.0625 to 0.0625
- vector_second: float32 [12, 768], replicated, may hold values from 1.4e-06 to 5.7e-06
Outputs:
- block_out: float32 [49152, 768], P(('rows', 'heads'))
- grad_in: float32 [49152, 768], P(('rows', 'heads'))
- grad_norm: float32 [1], replicated
- qkv_new: float32 [3, 768, 768], P(None, 'rows', 'heads')
- qkv_first_new: float32 [3, 768, 768], P(None, 'rows', 'heads')
- qkv_second_new: float32 [3, 768, 768], P(None, 'rows', 'heads')
- out_new: float32 [768, 768], P(('rows', 'heads'))
- out_first_new: float32 [768, 768], P(('rows', 'heads'))
- out_second_new: float32 [768, 768], P(('rows', 'heads'))
- in_new: float32 [768, 3072], P(('rows', 'heads'))
- in_first_new: float32 [768, 3072], P(('rows', 'heads'))
- in_second_new: float32 [768, 3072], P(('rows', 'heads'))
- back_new: float32 [3072, 768], P(('rows', 'heads'))
- back_first_new: float32 [3072, 768], P(('rows', 'heads'))
- back_second_new: float32 [3072, 768], P(('rows', 'heads'))
- vectors_new: float32 [12, 768], replicated
- vector_first_new: float32 [12, 768], replicated
- vector_second_new: float32 [12, 768], replicated
Inputs may be any that keep to these rules, and one draw needn't show every extreme that they name: Each sequence's keys at positions lengths[i] and beyond are masked; the longest sequence has exactly 512. `vectors`: rows 3 and 6 are the norms' gains, the other rows biases.
All inputs are finite; a program needn't handle non-finite values. No bound on the sum of `lengths` on one device may be relied on, other than what follows from the above.
Results may differ from a plain program's by a relative error of at most 0.015.
The roundings to bfloat16 on the way count: a program that leaves them out, or rounds other values in their place, can miss the bound.
Values may be sent and summed in bfloat16 or wider, within the bound.
No kernel may reach another device: no remote copies, remote signals or barrier semaphores. Data moves between devices by JAX's collectives and lax.ppermute only.
A program may use at most 192 MiB of HBM per device.

v0:
```python
import jax
import jax.numpy as jnp
from jax import lax
from jax.sharding import PartitionSpec as P

HEAD_DIM = 64
eps_norm = 1e-12
clip_limit = 100.0
learn_rate = 0.08
vector_rate = 0.3
beta_one = 0.9
beta_two = 0.999
adam_eps = 1e-06
decay_rate = 0.01
step_count = 10


def layer_norm(values, gain, shift):
    center = values - jnp.mean(values, axis=-1, keepdims=True)
    spread = jnp.mean(center * center, axis=-1, keepdims=True)
    return center * lax.rsqrt(spread + eps_norm) * gain + shift


def gelu_exact(values):
    return jax.nn.gelu(values, approximate=False)


def masked_scores(queries, key_rows, length):
    scores = jnp.einsum(
        "qhe,khe->hqk", queries, key_rows, preferred_element_type=jnp.float32
    ) * HEAD_DIM ** (-0.5)
    places = lax.broadcasted_iota(jnp.int32, (1, 1, scores.shape[2]), 2)
    return jnp.where(places < length, scores, -1000000000.0)


def attend_forward(item):
    queries, key_rows, value_rows, length = item
    scores = masked_scores(queries, key_rows, length)
    highest = jnp.max(scores, axis=2, keepdims=True)
    weights = jnp.exp(scores - highest)
    total = jnp.sum(weights, axis=2, keepdims=True)
    probs = (weights / total).astype(jnp.bfloat16)
    context = jnp.einsum("hqk,khe->qhe", probs, value_rows, preferred_element_type=jnp.float32)
    return (context.astype(jnp.bfloat16), highest + jnp.log(total))


def attend_backward(item):
    queries, key_rows, value_rows, length, log_total, grad_context = item
    scores = masked_scores(queries, key_rows, length)
    probs = jnp.exp(scores - log_total)
    grad_value = jnp.einsum(
        "hqk,qhe->khe", probs.astype(jnp.bfloat16), grad_context, preferred_element_type=jnp.float32
    )
    grad_probs = jnp.einsum(
        "qhe,khe->hqk", grad_context, value_rows, preferred_element_type=jnp.float32
    )
    grad_scores = probs * (grad_probs - jnp.sum(probs * grad_probs, axis=2, keepdims=True))
    grad_scores = grad_scores.astype(jnp.bfloat16)
    scaling = HEAD_DIM ** (-0.5)
    grad_query = (
        jnp.einsum("hqk,khe->qhe", grad_scores, key_rows, preferred_element_type=jnp.float32)
        * scaling
    )
    grad_key = (
        jnp.einsum("hqk,qhe->khe", grad_scores, queries, preferred_element_type=jnp.float32)
        * scaling
    )
    return (
        grad_query.astype(jnp.bfloat16),
        grad_key.astype(jnp.bfloat16),
        grad_value.astype(jnp.bfloat16),
    )


def adam_update(weight, first, second, grad, decay, rate):
    first_new = beta_one * first + (1.0 - beta_one) * grad
    second_new = beta_two * second + (1.0 - beta_two) * grad * grad
    fix_one = 1.0 - beta_one**step_count
    fix_two = 1.0 - beta_two**step_count
    move = first_new / fix_one / (jnp.sqrt(second_new / fix_two) + adam_eps)
    return (weight - rate * (move + decay * weight), first_new, second_new)


def body(
    tokens,
    cotangent,
    lengths,
    qkv_weight,
    qkv_first,
    qkv_second,
    out_weight,
    out_first,
    out_second,
    in_weight,
    in_first,
    in_second,
    back_weight,
    back_first,
    back_second,
    vectors,
    vector_first,
    vector_second,
):
    head_index = lax.axis_index("heads")
    local = qkv_weight.shape[2]
    model = tokens.shape[1]
    tok_all = tokens.shape[0]
    tok_half = cotangent.shape[0]
    seq_count = lengths.shape[0]
    seq_len = tok_all // seq_count
    loc_heads = local // HEAD_DIM
    qkv_full = lax.all_gather(qkv_weight.astype(jnp.bfloat16), "rows", axis=1, tiled=True)
    out_full, in_full, back_full = (
        lax.all_gather(out_weight.astype(jnp.bfloat16), ("rows", "heads"), axis=0, tiled=True),
        lax.all_gather(in_weight.astype(jnp.bfloat16), ("rows", "heads"), axis=0, tiled=True),
        lax.all_gather(back_weight.astype(jnp.bfloat16), ("rows", "heads"), axis=0, tiled=True),
    )
    bias_query = lax.dynamic_slice_in_dim(vectors[0], head_index * local, local)
    bias_value = lax.dynamic_slice_in_dim(vectors[1], head_index * local, local)
    bias_inner = vectors[8:].reshape(-1)
    projected = jnp.einsum("td,jdc->jtc", tokens, qkv_full, preferred_element_type=jnp.float32)
    queries = (projected[0] + bias_query).astype(jnp.bfloat16)
    key_rows = projected[1].astype(jnp.bfloat16)
    value_rows = (projected[2] + bias_value).astype(jnp.bfloat16)

    def per_seq(array):
        return array.reshape(seq_count, seq_len, loc_heads, HEAD_DIM)

    seq_query = per_seq(queries)
    seq_key = per_seq(key_rows)
    seq_value = per_seq(value_rows)
    context, log_totals = lax.map(attend_forward, (seq_query, seq_key, seq_value, lengths))
    context = context.reshape(tok_all, local)
    ctx_tokens = lax.all_to_all(context, "heads", split_axis=0, concat_axis=1, tiled=True)
    x_half = lax.dynamic_slice_in_dim(tokens, head_index * tok_half, tok_half, 0).astype(
        jnp.float32
    )
    attn_out = jnp.dot(ctx_tokens, out_full, preferred_element_type=jnp.float32) + vectors[2]
    hidden, norm_one_pull = jax.vjp(layer_norm, x_half + attn_out, vectors[3], vectors[4])
    hidden_low = hidden.astype(jnp.bfloat16)
    inner = jnp.dot(hidden_low, in_full, preferred_element_type=jnp.float32) + bias_inner
    activ, gelu_pull = jax.vjp(gelu_exact, inner)
    activ_low = activ.astype(jnp.bfloat16)
    ffn_out = jnp.dot(activ_low, back_full, preferred_element_type=jnp.float32) + vectors[5]
    block_out, norm_two_pull = jax.vjp(layer_norm, hidden + ffn_out, vectors[6], vectors[7])
    grad_second, grad_gain_two, grad_shift_two = norm_two_pull(cotangent.astype(jnp.float32))
    grad_ffn = grad_second.astype(jnp.bfloat16)
    grad_back = jnp.dot(activ_low.T, grad_ffn, preferred_element_type=jnp.float32)
    grad_activ = jnp.dot(grad_ffn, back_full.T, preferred_element_type=jnp.float32)
    grad_inner = gelu_pull(grad_activ)[0].astype(jnp.bfloat16)
    grad_in_w = jnp.dot(hidden_low.T, grad_inner, preferred_element_type=jnp.float32)
    grad_hidden = grad_second + jnp.dot(grad_inner, in_full.T, preferred_element_type=jnp.float32)
    grad_first, grad_gain_one, grad_shift_one = norm_one_pull(grad_hidden)
    grad_attn = grad_first.astype(jnp.bfloat16)
    grad_out_w = jnp.dot(ctx_tokens.T, grad_attn, preferred_element_type=jnp.float32)
    grad_ctx = jnp.dot(grad_attn, out_full.T, preferred_element_type=jnp.float32).astype(
        jnp.bfloat16
    )
    grad_context = lax.all_to_all(grad_ctx, "heads", split_axis=1, concat_axis=0, tiled=True)
    grad_query, grad_key, grad_value = lax.map(
        attend_backward, (seq_query, seq_key, seq_value, lengths, log_totals, per_seq(grad_context))
    )
    grad_stack = jnp.stack(
        [
            grad_query.reshape(tok_all, local),
            grad_key.reshape(tok_all, local),
            grad_value.reshape(tok_all, local),
        ]
    )
    grad_qkv = jnp.einsum("td,jtc->jdc", tokens, grad_stack, preferred_element_type=jnp.float32)
    grad_tokens = jnp.einsum(
        "jtc,jdc->td", grad_stack, qkv_full, preferred_element_type=jnp.float32
    )
    grad_in = grad_first + lax.psum_scatter(
        grad_tokens.astype(jnp.bfloat16), "heads", scatter_dimension=0, tiled=True
    ).astype(jnp.float32)
    qkv_grad = lax.psum_scatter(grad_qkv, "rows", scatter_dimension=1, tiled=True)
    out_grad, in_grad, back_grad = (
        lax.psum_scatter(grad_out_w, ("rows", "heads"), scatter_dimension=0, tiled=True),
        lax.psum_scatter(grad_in_w, ("rows", "heads"), scatter_dimension=0, tiled=True),
        lax.psum_scatter(grad_back, ("rows", "heads"), scatter_dimension=0, tiled=True),
    )
    zero_row = jnp.zeros((model,), jnp.float32)
    row_query = lax.dynamic_update_slice_in_dim(
        zero_row, jnp.sum(grad_stack[0].astype(jnp.float32), axis=0), head_index * local, 0
    )
    row_value = lax.dynamic_update_slice_in_dim(
        zero_row, jnp.sum(grad_stack[2].astype(jnp.float32), axis=0), head_index * local, 0
    )
    vector_part = jnp.concatenate(
        [
            row_query[None],
            row_value[None],
            jnp.sum(grad_attn.astype(jnp.float32), axis=0)[None],
            grad_gain_one[None],
            grad_shift_one[None],
            jnp.sum(grad_ffn.astype(jnp.float32), axis=0)[None],
            grad_gain_two[None],
            grad_shift_two[None],
            jnp.sum(grad_inner.astype(jnp.float32), axis=0).reshape(-1, model),
        ],
        axis=0,
    )
    square_part = (
        jnp.sum(qkv_grad * qkv_grad)
        + jnp.sum(out_grad * out_grad)
        + jnp.sum(in_grad * in_grad)
        + jnp.sum(back_grad * back_grad)
    )
    vector_grad, square_total = lax.psum((vector_part, square_part), ("rows", "heads"))
    grad_norm = jnp.sqrt(square_total + jnp.sum(vector_grad * vector_grad))
    factor = clip_limit / jnp.maximum(grad_norm, clip_limit)
    qkv_new = adam_update(
        qkv_weight, qkv_first, qkv_second, factor * qkv_grad, decay_rate, learn_rate
    )
    out_new = adam_update(
        out_weight, out_first, out_second, factor * out_grad, decay_rate, learn_rate
    )
    in_new = adam_update(in_weight, in_first, in_second, factor * in_grad, decay_rate, learn_rate)
    back_new = adam_update(
        back_weight, back_first, back_second, factor * back_grad, decay_rate, learn_rate
    )
    vec_new = adam_update(
        vectors, vector_first, vector_second, factor * vector_grad, 0.0, vector_rate
    )
    return (
        block_out,
        grad_in,
        grad_norm.reshape(1),
        qkv_new[0],
        qkv_new[1],
        qkv_new[2],
        out_new[0],
        out_new[1],
        out_new[2],
        in_new[0],
        in_new[1],
        in_new[2],
        back_new[0],
        back_new[1],
        back_new[2],
        vec_new[0],
        vec_new[1],
        vec_new[2],
    )


def solution(mesh):
    in_specs = (
        P("rows", None),
        P(("rows", "heads"), None),
        P("rows"),
        P(None, "rows", "heads"),
        P(None, "rows", "heads"),
        P(None, "rows", "heads"),
        P(("rows", "heads"), None),
        P(("rows", "heads"), None),
        P(("rows", "heads"), None),
        P(("rows", "heads"), None),
        P(("rows", "heads"), None),
        P(("rows", "heads"), None),
        P(("rows", "heads"), None),
        P(("rows", "heads"), None),
        P(("rows", "heads"), None),
        P(),
        P(),
        P(),
    )
    out_specs = (
        P(("rows", "heads"), None),
        P(("rows", "heads"), None),
        P(),
        P(None, "rows", "heads"),
        P(None, "rows", "heads"),
        P(None, "rows", "heads"),
        P(("rows", "heads"), None),
        P(("rows", "heads"), None),
        P(("rows", "heads"), None),
        P(("rows", "heads"), None),
        P(("rows", "heads"), None),
        P(("rows", "heads"), None),
        P(("rows", "heads"), None),
        P(("rows", "heads"), None),
        P(("rows", "heads"), None),
        P(),
        P(),
        P(),
    )
    return jax.shard_map(body, mesh=mesh, in_specs=in_specs, out_specs=out_specs, check_vma=False)
```

profile of v0, /device:TPU:0, one launch (start us, length us, event | category | flops | bytes accessed | tf_op | source)
XLA Modules:
  0.0 1076.9 jit_solution(10501911551029216793)
XLA Ops:
  20.1 4.3 copy.140
  24.4 48.6 %all-gather.5.cloned.1.call-done = bf16[3,768,384]{2,1,0:T(8,128)(2,1)} async-done(((bf16[3,48,384]{2,1,0:T(8,128)(2,1)}), bf16[3,768,384]{2,1,0:T(8,128)(2,1)}) %all-gather.5.cloned.1.call-update) | async-done | bytes 1769488 | tf_op jit(solution)/shard_map/all_gather | solution.py:112
  73.0 8.2 convolution_bitcast_fusion
  81.2 4.4 fusion.95
  87.3 7.4 squeeze.40
  94.7 3.1 add_convert_fusion.2
  100.0 7.4 squeeze.41
  107.4 3.1 add_convert_fusion.1
  111.3 6.0 convert_element_type.109
  117.4 4.1 copy.137
  123.2 55.7 %while.26 = (s32[]{:T(128)}, bf16[6,512,6,64]{1,3,2,0:T(8,128)(2,1)}, f32[6,6,512,1]{2,1,3,0:T(8,128)}, bf16[6,512,6,64]{1,3,2,0:T(8,128)(2,1)}, s32[6]{0:T(128)...) while((s32[]{:T(128)}, bf16[6,512,6,64]{1,3,2,0:T(8,128)(2,1)}, ...), condition=%wide.region_3.4_spmd, body=%wide.region_0.3_spmd.sunk | while | flops 421721600 | bytes 20554340 | solution.py:132
  129.1 3.5 fusion.143
  138.3 3.5 fusion.143
  147.5 3.5 fusion.143
  156.8 3.5 fusion.143
  166.0 3.5 fusion.143
  175.2 3.6 fusion.143
  178.8 5.7 copy.138
  184.5 6.8 all_to_all.26
  191.3 3.3 copy.139
  194.7 5.0 all-to-all-start
  202.9 4.4 fusion.96
  210.3 49.8 %multiply_convert_fusion.1 = (bf16[1536,3072]{1,0:T(8,128)(2,1)}, f32[1536,3072]{1,0:T(8,128)}, f32[1536,3072]{1,0:T(8,128)}) fusion(f32[3072]{0:T(1024)S(1)} %add.251, bf16[768,3072]{1,0:T(8,128)(2,1)} %all-gather.9.cloned.1.call-done, bf16[1536,768]{0,1:T(8,128)(2,1)S(1)} %fusion.86.clone.4), kind=kOutput, calls=%fused_computation.68 | convolution fusion | flops 7559184384 | bytes 54276096 | tf_op jit(solution)/shard_map/dot_general | solution.py:141
  261.3 13.6 %fusion.97 = (f32[1536]{0:T(1024)S(1)}, f32[1536,768]{0,1:T(8,128)S(1)}) fusion(f32[768]{0:T(1024)S(1)} %copy-done.36, bf16[1536,3072]{1,0:T(8,128)(2,1)} %get-tuple-element.328, bf16[3072,768]{1,0:T(8,128)(2,1)} %all-gather.11.cloned.1.call-done, f32[768]{0:T(1024)S(1)} %get-tuple-element.265, f32[768]{0:T(1024)S(1)} %get-tuple-element.266, ...), kind=kOutput, calls=%fused_computation.175 | convolution fusion | flops 7256013312 | bytes 23620608 | tf_op jit(solution)/shard_map/dot_general | solution.py:144
  280.2 5.4 convert_reduce_fusion.2
  285.6 26.8 %convert_reduce_fusion = (f32[3072]{0:T(1024)}, bf16[1536,3072]{1,0:T(8,128)(2,1)}) fusion(f32[1536,3072]{1,0:T(8,128)} %get-tuple-element.329, bf16[1536,768]{0,1:T(8,128)(2,1)} %get-tuple-element.321, bf16[3072,768]{1,0:T(8,128)(2,1)} %all-gather.11.cloned.1.call-done, f32[1536,3072]{1,0:T(8,128)} %get-tuple-element.343, f32[3072]{0:T(1024)S(1)} %add.251), kind=kOutput, calls=%fused_computation.66 | convolution fusion | flops 7327970304 | bytes 54288384 | tf_op jit(solution)/shard_map/dot_general | solution.py:149
  312.4 14.9 %multiply_reduce_fusion.1 = (f32[768]{0:T(1024)}, f32[1536]{0:T(1024)S(1)}, f32[768]{0:T(1024)}, f32[1536,768]{0,1:T(8,128)S(1)}) fusion(f32[1536,768]{0,1:T(8,128)S(1)} %bitcast.160, f32[1536]{0:T(1024)S(1)} %fusion.81, f32[1536]{0:T(1024)S(1)} %broadcast_multiply_fusion.1, f32[768]{0:T(1024)S(1)} %get-tuple-element.266, ...), kind=kOutput, calls=%fused_computation.100 | convolution fusion | flops 7267808256 | bytes 30726144 | tf_op jit(solution)/shard_map/dot_general | solution.py:152
  331.9 5.1 fusion.98
  337.0 3.3 convolution_convert_fusion
  340.3 5.6 all_to_all.35
  345.9 3.8 copy.142
  349.7 5.7 reshape.186
  361.3 104.7 %while.27 = (s32[]{:T(128)}, bf16[6,512,6,64]{1,3,2,0:T(8,128)(2,1)S(1)}, bf16[6,512,6,64]{1,3,2,0:T(8,128)(2,1)}, bf16[6,512,6,64]{1,3,2,0:T(8,128)(2,1)}, bf16...) while((s32[]{:T(128)}, ...), condition=%wide.region_14.15_spmd, body=%wide.region_12.14_spmd.sunk | while | flops 1031206400 | bytes 51211392 | solution.py:160
  365.7 3.3 multiply_reduce_fusion.11
  375.6 3.4 fusion.155
  383.1 3.3 multiply_reduce_fusion.11
  393.0 3.4 fusion.155
  400.5 3.3 multiply_reduce_fusion.11
  410.4 3.4 fusion.155
  417.9 3.3 multiply_reduce_fusion.11
  427.8 3.4 fusion.155
  435.3 3.3 multiply_reduce_fusion.11
  445.2 3.4 fusion.155
  452.7 3.3 multiply_reduce_fusion.11
  462.6 3.4 fusion.155
  466.0 6.0 copy.166
  472.0 8.7 reshape.195
  480.7 7.7 copy.167
  488.4 8.7 reshape.196
  497.2 7.7 copy.168
  504.8 9.1 reshape.197
  520.5 7.7 fusion.73
  528.1 6.3 copy.155
  534.5 10.5 bitcast_convert_fusion
  545.7 13.8 %fusion.83 = f32[768,3072]{1,0:T(8,128)} fusion(bf16[1536,3072]{1,0:T(8,128)(2,1)} %get-tuple-element.348, f32[1536,768]{0,1:T(8,128)} %copy-done.1, f32[768]{0:T(1024)S(1)} %copy-done.30, f32[768]{0:T(1024)S(1)} %get-tuple-element.266, f32[1536]{0:T(1024)S(1)} %fusion.81, f32[1536]{0:T(1024)S(1)} %broadcast_multiply_fusion.1), kind=kOutput, calls=%fused_computation.169 | convolution fusion | flops 7253655552 | bytes 23611392 | tf_op jit(solution)/shard_map/dot_general | solution.py:151
  559.6 13.3 %fusion.99 = f32[3072,768]{1,0:T(8,128)} fusion(bf16[1536,3072]{1,0:T(8,128)(2,1)} %get-tuple-element.328, bf16[1536,768]{0,1:T(8,128)(2,1)} %get-tuple-element.321), kind=kOutput, calls=%fused_computation.177 | convolution fusion | flops 7247757312 | bytes 21233664 | tf_op jit(solution)/shard_map/dot_general | solution.py:148
  577.6 6.1 copy.157
  585.3 127.9 %all-reduce.4.cloned.1.call-done = f32[3,768,384]{2,0,1:T(4,128)} async-done(((f32[3,768,384]{2,0,1:T(4,128)}), f32[3,768,384]{2,0,1:T(4,128)}) %all-reduce.4.cloned.1.call-update) | async-done | bytes 3538960
  716.2 11.0 %reduce-scatter.5.cloned.1.call-done = bf16[1536,768]{0,1:T(8,128)(2,1)} async-done(((bf16[3072,768]{0,1:T(8,128)(2,1)}), bf16[1536,768]{0,1:T(8,128)(2,1)}) %reduce-scatter.5.cloned.1.call-update) | async-done | bytes 2359312 | tf_op jit(solution)/shard_map/reduce_scatter | solution.py:174
  727.2 6.0 convert_add_fusion
  733.2 137.7 %reduce-scatter.9.cloned.1.call-done = f32[24,3072]{1,0:T(8,128)} async-done(((f32[768,3072]{1,0:T(8,128)}), f32[24,3072]{1,0:T(8,128)}) %reduce-scatter.9.cloned.1.call-update) | async-done | bytes 294928 | tf_op jit(solution)/shard_map/reduce_scatter | solution.py:180
  873.2 138.3 %reduce-scatter.11.cloned.1.call-done = f32[96,768]{1,0:T(8,128)} async-done(((f32[3072,768]{1,0:T(8,128)}), f32[96,768]{1,0:T(8,128)}) %reduce-scatter.11.cloned.1.call-update) | async-done | bytes 294928 | tf_op jit(solution)/shard_map/reduce_scatter | solution.py:181
  1013.9 6.2 copy.158
  1020.1 40.7 %all-reduce.1 = (f32[]{:T(128)}, f32[12,768]{1,0:T(8,128)}) all-reduce(f32[]{:T(128)S(6)} %add.266, f32[12,768]{1,0:T(8,128)S(1)} %concatenate.3), channel_id=1, replica_groups=mesh['rows'=16,'heads'=2] {'rows','heads'}, use_global_device_ids=true, to_apply=%region_24.25 | all-reduce | flops 9217 | bytes 73736 | tf_op jit(solution)/shard_map/psum | solution.py:210
  (254 shorter events, 165.7 us)
Async XLA Ops:
  7.2 65.8 %all-gather.5.cloned.1.call-start = ((), (), s32[]{:S(2)}) async-start(), calls=%async_computation.6 | async-start | bytes 1880064 | tf_op jit(solution)/shard_map/all_gather | solution.py:112
  8.9 190.9 %all-gather.7.cloned.1.call-start = ((), (), s32[]{:S(2)}) async-start(), calls=%async_computation.7 | async-start | bytes 1216512 | tf_op jit(solution)/shard_map/all_gather | solution.py:114
  10.4 199.9 %all-gather.9.cloned.1.call-start = ((), (), s32[]{:S(2)}) async-start(), calls=%async_computation.8 | async-start | bytes 4866048 | tf_op jit(solution)/shard_map/all_gather | solution.py:115
  12.2 249.2 %all-gather.11.cloned.1.call-start = ((), (), s32[]{:S(2)}) async-start(), calls=%async_computation.9 | async-start | bytes 4866048 | tf_op jit(solution)/shard_map/all_gather | solution.py:116
  15.6 245.8 %copy-start.29 = (f32[768]{0:T(1024)}, f32[768]{0:T(1024)S(1)}, u32[]{:S(2)}) copy-start(f32[768]{0:T(1024)S(1)} %get-tuple-element.265) | copy-start | bytes 9220
  15.8 4.3 slice-start.4
  117.3 5.8 copy-start.39
  178.8 12.5 %copy-start.3 = (bf16[6,512,6,64]{1,3,2,0:T(8,128)(2,1)}, bf16[6,512,6,64]{1,3,2,0:T(8,128)(2,1)S(1)}, u32[]{:S(2)}) copy-start(bf16[6,512,6,64]{1,3,2,0:T(8,128)(2,1)S(1)} %get-tuple-element.529) | copy-start | bytes 7077892
  194.7 8.2 copy-start.6
  194.7 8.2 all-to-all-start
  199.7 384.1 %reduce-scatter.7.cloned.1.call-start = ((), (), s32[]{:S(2)}) async-start(), calls=%async_computation.11 | async-start | bytes 2433024 | tf_op jit(solution)/shard_map/reduce_scatter | solution.py:179
  207.3 2.2 copy-start.1
  207.9 1.0 copy-start.21
  210.3 51.1 %copy-start.36 = (f32[768]{0:T(1024)S(1)}, f32[768]{0:T(1024)}, u32[]{:S(2)}) copy-start(f32[768]{0:T(1024)} %get-tuple-element.264) | copy-start | bytes 9220
  261.3 13.7 %copy-start.2 = (bf16[1536,768]{0,1:T(8,128)(2,1)S(1)}, bf16[1536,768]{0,1:T(8,128)(2,1)}, u32[]{:S(2)}) copy-start(bf16[1536,768]{0,1:T(8,128)(2,1)} %copy.140) | copy-start | bytes 7077892
  261.3 13.7 %copy-start.27 = (f32[768]{0:T(1024)S(1)}, f32[768]{0:T(1024)}, u32[]{:S(2)}) copy-start(f32[768]{0:T(1024)} %get-tuple-element.263) | copy-start | bytes 9220
  277.1 3.1 copy-start.31
  280.2 32.2 %slice-start = ((s8[4718592]{0:T(1024)(128)(4,1)}), s8[4194304]{0:T(1024)(128)(4,1)S(1)}, s32[]{:S(2)}) async-start(s8[4718592]{0:T(1024)(128)(4,1)} %bitcast.159), calls=%async_computation.15 | async-start | bytes 8388608
  285.6 26.8 %slice-start.1 = ((s8[4718592]{0:T(1024)(128)(4,1)}), s8[524288]{0:T(1024)(128)(4,1)S(1)}, s32[]{:S(2)}) async-start(s8[4718592]{0:T(1024)(128)(4,1)} %bitcast.159), calls=%async_computation.16 | async-start | bytes 1048576
  312.4 14.9 %copy-start.22 = (f32[1536]{0:T(1024)S(1)}, f32[1536]{0:T(1024)}, u32[]{:S(2)}) copy-start(f32[1536]{0:T(1024)} %copy-done.21) | copy-start | bytes 18436
  328.7 2.2 copy-start
  328.7 8.3 copy-start.25
  357.6 3.7 copy-start.40
  357.6 355.5 %all-reduce.4.cloned.1.call-start = ((), (), s32[]{:S(2)}) async-start(), calls=%async_computation.14 | async-start | bytes 9437184
  514.0 2.4 copy-start.4
  514.0 3.1 copy-start.5
  514.0 6.5 slice-start.2
  516.4 4.1 slice-start.3
  517.5 2.9 copy-start.12
  534.5 192.7 %reduce-scatter.5.cloned.1.call-start = ((), (), s32[]{:S(2)}) async-start(), calls=%async_computation.10 | async-start | bytes 7077888 | tf_op jit(solution)/shard_map/reduce_scatter | solution.py:174
  545.0 0.7 copy-start.30
  545.1 325.8 %reduce-scatter.9.cloned.1.call-start = ((), (), s32[]{:S(2)}) async-start(), calls=%async_computation.12 | async-start | bytes 9732096 | tf_op jit(solution)/shard_map/reduce_scatter | solution.py:180
  559.6 451.9 %reduce-scatter.11.cloned.1.call-start = ((), (), s32[]{:S(2)}) async-start(), calls=%async_computation.13 | async-start | bytes 9732096 | tf_op jit(solution)/shard_map/reduce_scatter | solution.py:181
  572.9 0.7 copy-start.41
  572.9 4.5 copy-start.34
  573.0 4.5 copy-start.38
  573.0 4.5 copy-start.37
  573.0 4.5 copy-start.35
  573.0 4.6 copy-start.33
  573.0 4.6 copy-start.32
  573.0 4.6 copy-start.28
  577.6 149.6 %copy-start.26 = (f32[1536]{0:T(1024)S(1)}, f32[1536]{0:T(1024)}, u32[]{:S(2)}) copy-start(f32[1536]{0:T(1024)} %copy-done.25) | copy-start | bytes 18436
  1013.8 51.5 %copy-start.11 = (f32[3,48,384]{2,1,0:T(8,128)S(1)}, f32[3,48,384]{2,1,0:T(8,128)}, u32[]{:S(2)}) copy-start(f32[3,48,384]{2,1,0:T(8,128)} %param.25) | copy-start | bytes 663556
  1013.8 51.5 %copy-start.19 = (f32[3,48,384]{2,1,0:T(8,128)S(1)}, f32[3,48,384]{2,1,0:T(8,128)}, u32[]{:S(2)}) copy-start(f32[3,48,384]{2,1,0:T(8,128)} %param.26) | copy-start | bytes 663556
  1013.8 51.5 %copy-start.20 = (f32[3,48,384]{2,1,0:T(8,128)S(1)}, f32[3,48,384]{2,1,0:T(8,128)}, u32[]{:S(2)}) copy-start(f32[3,48,384]{2,1,0:T(8,128)} %param.27) | copy-start | bytes 663556
  1013.8 52.4 %copy-start.7 = (f32[96,768]{1,0:T(8,128)S(1)}, f32[96,768]{1,0:T(8,128)}, u32[]{:S(2)}) copy-start(f32[96,768]{1,0:T(8,128)} %param.34) | copy-start | bytes 884740
  1013.8 52.4 %copy-start.10 = (f32[96,768]{1,0:T(8,128)S(1)}, f32[96,768]{1,0:T(8,128)}, u32[]{:S(2)}) copy-start(f32[96,768]{1,0:T(8,128)} %reduce-scatter.11.cloned.1.call-done) | copy-start | bytes 884740
  1013.8 52.4 %copy-start.13 = (f32[96,768]{1,0:T(8,128)S(1)}, f32[96,768]{1,0:T(8,128)}, u32[]{:S(2)}) copy-start(f32[96,768]{1,0:T(8,128)} %param.35) | copy-start | bytes 884740
  1013.8 52.4 %copy-start.14 = (f32[96,768]{1,0:T(8,128)S(1)}, f32[96,768]{1,0:T(8,128)}, u32[]{:S(2)}) copy-start(f32[96,768]{1,0:T(8,128)} %param.36) | copy-start | bytes 884740
  1013.8 53.5 %copy-start.8 = (f32[24,3072]{1,0:T(8,128)S(1)}, f32[24,3072]{1,0:T(8,128)}, u32[]{:S(2)}) copy-start(f32[24,3072]{1,0:T(8,128)} %param.31) | copy-start | bytes 884740
  1013.8 53.4 %copy-start.9 = (f32[24,3072]{1,0:T(8,128)S(1)}, f32[24,3072]{1,0:T(8,128)}, u32[]{:S(2)}) copy-start(f32[24,3072]{1,0:T(8,128)} %reduce-scatter.9.cloned.1.call-done) | copy-start | bytes 884740
  1013.9 53.4 %copy-start.15 = (f32[24,3072]{1,0:T(8,128)S(1)}, f32[24,3072]{1,0:T(8,128)}, u32[]{:S(2)}) copy-start(f32[24,3072]{1,0:T(8,128)} %param.32) | copy-start | bytes 884740
  1013.9 53.4 %copy-start.16 = (f32[24,3072]{1,0:T(8,128)S(1)}, f32[24,3072]{1,0:T(8,128)}, u32[]{:S(2)}) copy-start(f32[24,3072]{1,0:T(8,128)} %param.33) | copy-start | bytes 884740
  1020.1 48.3 %copy-start.17 = (f32[24,768]{1,0:T(8,128)S(1)}, f32[24,768]{1,0:T(8,128)}, u32[]{:S(2)}) copy-start(f32[24,768]{1,0:T(8,128)} %param.28) | copy-start | bytes 221188
  1020.1 48.3 %copy-start.18 = (f32[24,768]{1,0:T(8,128)S(1)}, f32[24,768]{1,0:T(8,128)}, u32[]{:S(2)}) copy-start(f32[24,768]{1,0:T(8,128)} %reduce-scatter.7.cloned.1.call-done) | copy-start | bytes 221188
  1060.8 7.6 copy-start.23
  1063.6 4.7 copy-start.24
Sparse Core Ops, SparseCore 0:
  11.3 61.6 all-gather.4
  76.4 52.7 all-gather.6
  132.8 62.5 all-gather.8
  198.7 62.6 all-gather.10
  357.8 97.8 reduce-scatter.6
  534.6 178.5 all-reduce.3
  715.5 11.6 reduce-scatter.4
  734.1 136.7 reduce-scatter.8
  876.8 134.5 reduce-scatter.10
where the time goes:
time: 1090 us; the launch traced here: 1080 us
  waiting for transfers between devices  468 us (43%)
  matrix products  287 us (26%)
  local copies, waits for them, and re-layouts  168 us (15%)
  other arithmetic  81.8 us (8%)
  blocking collectives  46.3 us (4%)
  between operations  20.4 us (2%)
    reduce_scatter x1, waiting for transfers between devices, body(): lax.psum_scatter(grad_back, ('rows', 'heads'), scatter_dimension=0, tiled...  138 us
    reduce_scatter x1, waiting for transfers between devices, body(): lax.psum_scatter(grad_in_w, ('rows', 'heads'), scatter_dimension=0, tiled...  138 us
    unnamed x10, waiting for transfers between devices  128 us
    dot_general x1, matrix products, body(): jnp.dot(hidden_low, in_full, preferred_element_type=jnp.float32)  49.8 us
    all_gather x1, waiting for transfers between devices, body(): lax.all_gather(qkv_weight.astype(jnp.bfloat16), 'rows', axis=1, tiled=True)  48.6 us
    another operation x7, local copies, waits for them, and re-layouts, body(): jnp.stack([grad_query.reshape(tok_all, local), grad_key.reshape(tok_all,...  48.4 us
    psum x1, blocking collectives, body(): lax.psum((vector_part, square_part), ('rows', 'heads'))  40.7 us
    unnamed x99, local copies, waits for them, and re-layouts  30.7 us
  transfers between devices with their start and end apart: 10, of which 7 were waited for; matrix products, arithmetic and copies ran while one was open for 39% of the time, Pallas kernels for 0%

commit v1 on v0

--- a/solution.py
+++ b/solution.py
@@ -207,7 +207,7 @@
         + jnp.sum(in_grad * in_grad)
         + jnp.sum(back_grad * back_grad)
     )
-    vector_grad, square_total = lax.psum((vector_part, square_part), ("rows", "heads"))
+    vector_grad, square_total = lax.psum(lax.psum((vector_part, square_part), "heads"), "rows")
     grad_norm = jnp.sqrt(square_total + jnp.sum(vector_grad * vector_grad))
     factor = clip_limit / jnp.maximum(grad_norm, clip_limit)
     qkv_new = adam_update(

time: 1090 us -> 1130 us (1.037)
  blocking collectives: 46.3 us -> 85.3 us
    psum x1 -> x2, blocking collectives: 40.7 us -> 79.7 us  [the longest x1 75.5 us: body(): lax.psum(lax.psum((vector_part, square_part), 'heads'), 'rows')]
  transfers between devices with their start and end apart: 10 -> 10, of which waited for: 7 -> 7; matrix products, arithmetic and copies ran while one was open for 39% -> 37% of each run, Pallas kernels for 0% -> 0%
where the time goes in v1:
time: 1130 us; the launch traced here: 1120 us
  waiting for transfers between devices  468 us (41%)
  matrix products  287 us (25%)
  local copies, waits for them, and re-layouts  168 us (15%)
  blocking collectives  85.3 us (8%)
  other arithmetic  80.9 us (7%)
  between operations  20.4 us (2%)
    reduce_scatter x1, waiting for transfers between devices, body(): lax.psum_scatter(grad_back, ('rows', 'heads'), scatter_dimension=0, tiled...  138 us
    reduce_scatter x1, waiting for transfers between devices, body(): lax.psum_scatter(grad_in_w, ('rows', 'heads'), scatter_dimension=0, tiled...  138 us
    unnamed x10, waiting for transfers between devices  128 us
    psum x1, blocking collectives, body(): lax.psum(lax.psum((vector_part, square_part), 'heads'), 'rows')  75.5 us
    dot_general x1, matrix products, body(): jnp.dot(hidden_low, in_full, preferred_element_type=jnp.float32)  49.8 us
    all_gather x1, waiting for transfers between devices, body(): lax.all_gather(qkv_weight.astype(jnp.bfloat16), 'rows', axis=1, tiled=True)  48.6 us
    another operation x7, local copies, waits for them, and re-layouts, body(): jnp.stack([grad_query.reshape(tok_all, local), grad_key.reshape(tok_all,...  48.4 us
    unnamed x99, local copies, waits for them, and re-layouts  30.7 us
  transfers between devices with their start and end apart: 10, of which 7 were waited for; matrix products, arithmetic and copies ran while one was open for 37% of the time, Pallas kernels for 0%

profile of v1, /device:TPU:0, one launch (start us, length us, event | category | flops | bytes accessed | tf_op | source)
XLA Modules:
  0.0 1115.1 jit_solution(9641128455446315014)
XLA Ops:
  20.1 4.3 copy.140
  24.4 48.6 %all-gather.5.cloned.1.call-done = bf16[3,768,384]{2,1,0:T(8,128)(2,1)} async-done(((bf16[3,48,384]{2,1,0:T(8,128)(2,1)}), bf16[3,768,384]{2,1,0:T(8,128)(2,1)}) %all-gather.5.cloned.1.call-update) | async-done | bytes 1769488 | tf_op jit(solution)/shard_map/all_gather | solution.py:112
  73.0 8.2 convolution_bitcast_fusion
  81.2 4.4 fusion.95
  87.3 7.4 squeeze.40
  100.0 7.4 squeeze.41
  107.4 3.1 add_convert_fusion.1
  111.3 6.0 convert_element_type.109
  117.4 4.1 copy.137
  123.2 55.7 %while.26 = (s32[]{:T(128)}, bf16[6,512,6,64]{1,3,2,0:T(8,128)(2,1)}, f32[6,6,512,1]{2,1,3,0:T(8,128)}, bf16[6,512,6,64]{1,3,2,0:T(8,128)(2,1)}, s32[6]{0:T(128)...) while((s32[]{:T(128)}, bf16[6,512,6,64]{1,3,2,0:T(8,128)(2,1)}, ...), condition=%wide.region_3.4_spmd, body=%wide.region_0.3_spmd.sunk | while | flops 421721600 | bytes 20554340 | solution.py:132
  129.1 3.5 fusion.143
  138.3 3.5 fusion.143
  147.5 3.5 fusion.143
  156.8 3.5 fusion.143
  166.0 3.5 fusion.143
  175.2 3.6 fusion.143
  178.8 5.7 copy.138
  184.5 6.8 all_to_all.26
  191.3 3.3 copy.139
  194.7 5.0 all-to-all-start
  202.9 4.4 fusion.96
  210.3 49.8 %multiply_convert_fusion.1 = (bf16[1536,3072]{1,0:T(8,128)(2,1)}, f32[1536,3072]{1,0:T(8,128)}, f32[1536,3072]{1,0:T(8,128)}) fusion(f32[3072]{0:T(1024)S(1)} %add.255, bf16[768,3072]{1,0:T(8,128)(2,1)} %all-gather.9.cloned.1.call-done, bf16[1536,768]{0,1:T(8,128)(2,1)S(1)} %fusion.86.clone.4), kind=kOutput, calls=%fused_computation.68 | convolution fusion | flops 7559184384 | bytes 54276096 | tf_op jit(solution)/shard_map/dot_general | solution.py:141
  261.3 13.6 %fusion.97 = (f32[1536]{0:T(1024)S(1)}, f32[1536,768]{0,1:T(8,128)S(1)}) fusion(f32[768]{0:T(1024)S(1)} %copy-done.36, bf16[1536,3072]{1,0:T(8,128)(2,1)} %get-tuple-element.330, bf16[3072,768]{1,0:T(8,128)(2,1)} %all-gather.11.cloned.1.call-done, f32[768]{0:T(1024)S(1)} %get-tuple-element.265, f32[768]{0:T(1024)S(1)} %get-tuple-element.266, ...), kind=kOutput, calls=%fused_computation.175 | convolution fusion | flops 7256013312 | bytes 23620608 | tf_op jit(solution)/shard_map/dot_general | solution.py:144
  280.2 5.4 convert_reduce_fusion.2
  285.6 26.8 %convert_reduce_fusion = (f32[3072]{0:T(1024)}, bf16[1536,3072]{1,0:T(8,128)(2,1)}) fusion(f32[1536,3072]{1,0:T(8,128)} %get-tuple-element.331, bf16[1536,768]{0,1:T(8,128)(2,1)} %get-tuple-element.323, bf16[3072,768]{1,0:T(8,128)(2,1)} %all-gather.11.cloned.1.call-done, f32[1536,3072]{1,0:T(8,128)} %get-tuple-element.345, f32[3072]{0:T(1024)S(1)} %add.255), kind=kOutput, calls=%fused_computation.66 | convolution fusion | flops 7327970304 | bytes 54288384 | tf_op jit(solution)/shard_map/dot_general | solution.py:149
  312.4 14.9 %multiply_reduce_fusion.1 = (f32[768]{0:T(1024)}, f32[1536]{0:T(1024)S(1)}, f32[768]{0:T(1024)}, f32[1536,768]{0,1:T(8,128)S(1)}) fusion(f32[1536,768]{0,1:T(8,128)S(1)} %bitcast.160, f32[1536]{0:T(1024)S(1)} %fusion.81, f32[1536]{0:T(1024)S(1)} %broadcast_multiply_fusion.1, f32[768]{0:T(1024)S(1)} %get-tuple-element.266, ...), kind=kOutput, calls=%fused_computation.100 | convolution fusion | flops 7267808256 | bytes 30726144 | tf_op jit(solution)/shard_map/dot_general | solution.py:152
  331.9 5.1 fusion.98
  337.0 3.3 convolution_convert_fusion
  340.3 5.6 all_to_all.35
  345.9 3.8 copy.142
  349.7 5.7 reshape.186
  361.3 104.7 %while.27 = (s32[]{:T(128)}, bf16[6,512,6,64]{1,3,2,0:T(8,128)(2,1)S(1)}, bf16[6,512,6,64]{1,3,2,0:T(8,128)(2,1)}, bf16[6,512,6,64]{1,3,2,0:T(8,128)(2,1)}, bf16...) while((s32[]{:T(128)}, ...), condition=%wide.region_14.15_spmd, body=%wide.region_12.14_spmd.sunk | while | flops 1031206400 | bytes 51211392 | solution.py:160
  365.7 3.3 multiply_reduce_fusion.11
  375.6 3.4 fusion.155
  383.1 3.3 multiply_reduce_fusion.11
  393.0 3.4 fusion.155
  400.5 3.3 multiply_reduce_fusion.11
  410.4 3.4 fusion.155
  417.9 3.3 multiply_reduce_fusion.11
  427.8 3.4 fusion.155
  435.3 3.3 multiply_reduce_fusion.11
  445.2 3.4 fusion.155
  452.7 3.3 multiply_reduce_fusion.11
  462.6 3.4 fusion.155
  466.0 6.0 copy.166
  472.0 8.7 reshape.195
  480.7 7.7 copy.167
  488.4 8.7 reshape.196
  497.2 7.7 copy.168
  504.8 9.1 reshape.197
  520.5 7.7 fusion.73
  528.1 6.3 copy.155
  534.5 10.5 bitcast_convert_fusion
  545.7 13.8 %fusion.83 = f32[768,3072]{1,0:T(8,128)} fusion(bf16[1536,3072]{1,0:T(8,128)(2,1)} %get-tuple-element.350, f32[1536,768]{0,1:T(8,128)} %copy-done.1, f32[768]{0:T(1024)S(1)} %copy-done.30, f32[768]{0:T(1024)S(1)} %get-tuple-element.266, f32[1536]{0:T(1024)S(1)} %fusion.81, f32[1536]{0:T(1024)S(1)} %broadcast_multiply_fusion.1), kind=kOutput, calls=%fused_computation.169 | convolution fusion | flops 7253655552 | bytes 23611392 | tf_op jit(solution)/shard_map/dot_general | solution.py:151
  559.6 13.3 %fusion.99 = f32[3072,768]{1,0:T(8,128)} fusion(bf16[1536,3072]{1,0:T(8,128)(2,1)} %get-tuple-element.330, bf16[1536,768]{0,1:T(8,128)(2,1)} %get-tuple-element.323), kind=kOutput, calls=%fused_computation.177 | convolution fusion | flops 7247757312 | bytes 21233664 | tf_op jit(solution)/shard_map/dot_general | solution.py:148
  577.6 6.1 copy.157
  585.3 127.9 %all-reduce.5.cloned.1.call-done = f32[3,768,384]{2,0,1:T(4,128)} async-done(((f32[3,768,384]{2,0,1:T(4,128)}), f32[3,768,384]{2,0,1:T(4,128)}) %all-reduce.5.cloned.1.call-update) | async-done | bytes 3538960
  716.2 11.0 reduce-scatter.5.cloned.1.call-done
  727.2 6.0 convert_add_fusion
  733.2 137.7 %reduce-scatter.9.cloned.1.call-done = f32[24,3072]{1,0:T(8,128)} async-done(((f32[768,3072]{1,0:T(8,128)}), f32[24,3072]{1,0:T(8,128)}) %reduce-scatter.9.cloned.1.call-update) | async-done | bytes 294928 | tf_op jit(solution)/shard_map/reduce_scatter | solution.py:180
  873.2 138.3 %reduce-scatter.11.cloned.1.call-done = f32[96,768]{1,0:T(8,128)} async-done(((f32[3072,768]{1,0:T(8,128)}), f32[96,768]{1,0:T(8,128)}) %reduce-scatter.11.cloned.1.call-update) | async-done | bytes 294928 | tf_op jit(solution)/shard_map/reduce_scatter | solution.py:181
  1013.9 6.2 copy.158
  1020.1 4.3 all-reduce.2
  1024.4 75.5 %all-reduce.1 = (f32[]{:T(128)}, f32[12,768]{1,0:T(8,128)S(1)}) all-reduce(f32[]{:T(128)} %get-tuple-element.305, f32[12,768]{1,0:T(8,128)} %get-tuple-element.306), channel_id=1, replica_groups=mesh['rows'=16,'heads'=2] {'rows'}, use_global_device_ids=true, to_apply=%region_25.26 | all-reduce | flops 9217 | bytes 73736 | tf_op jit(solution)/shard_map/psum | solution.py:210
  (255 shorter events, 168.0 us)
Async XLA Ops:
  7.2 65.8 %all-gather.5.cloned.1.call-start = ((), (), s32[]{:S(2)}) async-start(), calls=%async_computation.6 | async-start | bytes 1880064 | tf_op jit(solution)/shard_map/all_gather | solution.py:112
  8.9 190.9 %all-gather.7.cloned.1.call-start = ((), (), s32[]{:S(2)}) async-start(), calls=%async_computation.7 | async-start | bytes 1216512 | tf_op jit(solution)/shard_map/all_gather | solution.py:114
  10.4 199.9 %all-gather.9.cloned.1.call-start = ((), (), s32[]{:S(2)}) async-start(), calls=%async_computation.8 | async-start | bytes 4866048 | tf_op jit(solution)/shard_map/all_gather | solution.py:115
  12.2 249.2 %all-gather.11.cloned.1.call-start = ((), (), s32[]{:S(2)}) async-start(), calls=%async_computation.9 | async-start | bytes 4866048 | tf_op jit(solution)/shard_map/all_gather | solution.py:116
  15.6 245.8 %copy-start.29 = (f32[768]{0:T(1024)}, f32[768]{0:T(1024)S(1)}, u32[]{:S(2)}) copy-start(f32[768]{0:T(1024)S(1)} %get-tuple-element.265) | copy-start | bytes 9220
  15.8 4.3 slice-start.4
  117.3 5.8 copy-start.39
  178.8 12.5 %copy-start.3 = (bf16[6,512,6,64]{1,3,2,0:T(8,128)(2,1)}, bf16[6,512,6,64]{1,3,2,0:T(8,128)(2,1)S(1)}, u32[]{:S(2)}) copy-start(bf16[6,512,6,64]{1,3,2,0:T(8,128)(2,1)S(1)} %get-tuple-element.531) | copy-start | bytes 7077892
  194.7 8.2 copy-start.6
  194.7 8.2 all-to-all-start
  199.7 384.1 %reduce-scatter.7.cloned.1.call-start = ((), (), s32[]{:S(2)}) async-start(), calls=%async_computation.11 | async-start | bytes 2433024 | tf_op jit(solution)/shard_map/reduce_scatter | solution.py:179
  207.3 2.2 copy-start.1
  207.9 1.0 copy-start.21
  210.3 51.1 %copy-start.36 = (f32[768]{0:T(1024)S(1)}, f32[768]{0:T(1024)}, u32[]{:S(2)}) copy-start(f32[768]{0:T(1024)} %get-tuple-element.264) | copy-start | bytes 9220
  261.3 13.7 %copy-start.2 = (bf16[1536,768]{0,1:T(8,128)(2,1)S(1)}, bf16[1536,768]{0,1:T(8,128)(2,1)}, u32[]{:S(2)}) copy-start(bf16[1536,768]{0,1:T(8,128)(2,1)} %copy.140) | copy-start | bytes 7077892
  261.3 13.7 %copy-start.27 = (f32[768]{0:T(1024)S(1)}, f32[768]{0:T(1024)}, u32[]{:S(2)}) copy-start(f32[768]{0:T(1024)} %get-tuple-element.263) | copy-start | bytes 9220
  277.1 3.1 copy-start.31
  280.2 32.2 %slice-start = ((s8[4718592]{0:T(1024)(128)(4,1)}), s8[4194304]{0:T(1024)(128)(4,1)S(1)}, s32[]{:S(2)}) async-start(s8[4718592]{0:T(1024)(128)(4,1)} %bitcast.159), calls=%async_computation.15 | async-start | bytes 8388608
  285.6 26.8 %slice-start.1 = ((s8[4718592]{0:T(1024)(128)(4,1)}), s8[524288]{0:T(1024)(128)(4,1)S(1)}, s32[]{:S(2)}) async-start(s8[4718592]{0:T(1024)(128)(4,1)} %bitcast.159), calls=%async_computation.16 | async-start | bytes 1048576
  312.4 14.9 %copy-start.22 = (f32[1536]{0:T(1024)S(1)}, f32[1536]{0:T(1024)}, u32[]{:S(2)}) copy-start(f32[1536]{0:T(1024)} %copy-done.21) | copy-start | bytes 18436
  328.7 2.2 copy-start
  328.7 8.3 copy-start.25
  357.6 3.7 copy-start.40
  357.6 355.5 %all-reduce.5.cloned.1.call-start = ((), (), s32[]{:S(2)}) async-start(), calls=%async_computation.14 | async-start | bytes 9437184
  514.0 2.4 copy-start.4
  514.0 3.1 copy-start.5
  514.0 6.5 slice-start.2
  516.4 4.1 slice-start.3
  517.5 2.9 copy-start.12
  534.5 192.7 %reduce-scatter.5.cloned.1.call-start = ((), (), s32[]{:S(2)}) async-start(), calls=%async_computation.10 | async-start | bytes 7077888 | tf_op jit(solution)/shard_map/reduce_scatter | solution.py:174
  545.0 0.7 copy-start.30
  545.1 325.8 %reduce-scatter.9.cloned.1.call-start = ((), (), s32[]{:S(2)}) async-start(), calls=%async_computation.12 | async-start | bytes 9732096 | tf_op jit(solution)/shard_map/reduce_scatter | solution.py:180
  559.6 451.9 %reduce-scatter.11.cloned.1.call-start = ((), (), s32[]{:S(2)}) async-start(), calls=%async_computation.13 | async-start | bytes 9732096 | tf_op jit(solution)/shard_map/reduce_scatter | solution.py:181
  572.9 0.7 copy-start.41
  572.9 4.5 copy-start.34
  573.0 4.5 copy-start.38
  573.0 4.5 copy-start.37
  573.0 4.5 copy-start.35
  573.0 4.6 copy-start.33
  573.0 4.6 copy-start.32
  573.0 4.6 copy-start.28
  577.6 149.6 %copy-start.26 = (f32[1536]{0:T(1024)S(1)}, f32[1536]{0:T(1024)}, u32[]{:S(2)}) copy-start(f32[1536]{0:T(1024)} %copy-done.25) | copy-start | bytes 18436
  1013.8 89.7 %copy-start.11 = (f32[3,48,384]{2,1,0:T(8,128)S(1)}, f32[3,48,384]{2,1,0:T(8,128)}, u32[]{:S(2)}) copy-start(f32[3,48,384]{2,1,0:T(8,128)} %param.25) | copy-start | bytes 663556
  1013.8 89.6 %copy-start.19 = (f32[3,48,384]{2,1,0:T(8,128)S(1)}, f32[3,48,384]{2,1,0:T(8,128)}, u32[]{:S(2)}) copy-start(f32[3,48,384]{2,1,0:T(8,128)} %param.26) | copy-start | bytes 663556
  1013.8 89.6 %copy-start.20 = (f32[3,48,384]{2,1,0:T(8,128)S(1)}, f32[3,48,384]{2,1,0:T(8,128)}, u32[]{:S(2)}) copy-start(f32[3,48,384]{2,1,0:T(8,128)} %param.27) | copy-start | bytes 663556
  1013.8 90.6 %copy-start.7 = (f32[96,768]{1,0:T(8,128)S(1)}, f32[96,768]{1,0:T(8,128)}, u32[]{:S(2)}) copy-start(f32[96,768]{1,0:T(8,128)} %param.34) | copy-start | bytes 884740
  1013.8 90.6 %copy-start.10 = (f32[96,768]{1,0:T(8,128)S(1)}, f32[96,768]{1,0:T(8,128)}, u32[]{:S(2)}) copy-start(f32[96,768]{1,0:T(8,128)} %reduce-scatter.11.cloned.1.call-done) | copy-start | bytes 884740
  1013.8 90.6 %copy-start.13 = (f32[96,768]{1,0:T(8,128)S(1)}, f32[96,768]{1,0:T(8,128)}, u32[]{:S(2)}) copy-start(f32[96,768]{1,0:T(8,128)} %param.35) | copy-start | bytes 884740
  1013.8 90.6 %copy-start.14 = (f32[96,768]{1,0:T(8,128)S(1)}, f32[96,768]{1,0:T(8,128)}, u32[]{:S(2)}) copy-start(f32[96,768]{1,0:T(8,128)} %param.36) | copy-start | bytes 884740
  1013.8 91.6 %copy-start.8 = (f32[24,3072]{1,0:T(8,128)S(1)}, f32[24,3072]{1,0:T(8,128)}, u32[]{:S(2)}) copy-start(f32[24,3072]{1,0:T(8,128)} %param.31) | copy-start | bytes 884740
  1013.8 91.6 %copy-start.9 = (f32[24,3072]{1,0:T(8,128)S(1)}, f32[24,3072]{1,0:T(8,128)}, u32[]{:S(2)}) copy-start(f32[24,3072]{1,0:T(8,128)} %reduce-scatter.9.cloned.1.call-done) | copy-start | bytes 884740
  1013.9 91.6 %copy-start.15 = (f32[24,3072]{1,0:T(8,128)S(1)}, f32[24,3072]{1,0:T(8,128)}, u32[]{:S(2)}) copy-start(f32[24,3072]{1,0:T(8,128)} %param.32) | copy-start | bytes 884740
  1013.9 91.6 %copy-start.16 = (f32[24,3072]{1,0:T(8,128)S(1)}, f32[24,3072]{1,0:T(8,128)}, u32[]{:S(2)}) copy-start(f32[24,3072]{1,0:T(8,128)} %param.33) | copy-start | bytes 884740
  1020.1 86.4 %copy-start.17 = (f32[24,768]{1,0:T(8,128)S(1)}, f32[24,768]{1,0:T(8,128)}, u32[]{:S(2)}) copy-start(f32[24,768]{1,0:T(8,128)} %param.28) | copy-start | bytes 221188
  1020.1 86.4 %copy-start.18 = (f32[24,768]{1,0:T(8,128)S(1)}, f32[24,768]{1,0:T(8,128)}, u32[]{:S(2)}) copy-start(f32[24,768]{1,0:T(8,128)} %reduce-scatter.7.cloned.1.call-done) | copy-start | bytes 221188
  1101.8 4.7 copy-start.23
  1101.8 4.7 copy-start.24
Sparse Core Ops, SparseCore 0:
  11.3 61.6 all-gather.4
  76.4 52.7 all-gather.6
  132.8 62.5 all-gather.8
  198.7 62.6 all-gather.10
  357.8 97.8 reduce-scatter.6
  534.6 178.5 all-reduce.4
  715.5 11.6 reduce-scatter.4
  734.1 136.7 reduce-scatter.8
  876.8 134.5 reduce-scatter.10
